TPU v7x, 256 devices: a whole 4x4x8 slice. The times are simulated.
256 devices in a mesh: seq: 4 (over x_lo, core), dp: 64 (over x_hi, y, z).
Axes of the slice: x: 4 (x_hi: 2, x_lo: 2; x = x_hi * 2 + x_lo), y: 4, z: 8, core: 2. Of those that a mesh axis runs over, the one named last changes fastest.
Arguments:
- residual: bfloat16 [49152, 2560], P(('seq', 'dp')), may hold values from -6 to 6
- query_raw: bfloat16 [49152, 2560], P(('seq', 'dp')), may hold values from -60 to 60
- key_raw: bfloat16 [49152, 2560], P(('seq', 'dp')), may hold values from -60 to 60
- values: bfloat16 [49152, 2560], P(('seq', 'dp')), may hold values from -6 to 6
- residual_grad: bfloat16 [49152, 2560], P(('seq', 'dp')), may hold values from -6 to 6
- modulated_grad: bfloat16 [49152, 2560], P(('seq', 'dp')), may hold values from -24 to 24
- condition: float32 [64, 2, 2560], P('dp'), may hold values from -3 to 3
- modulation: float32 [2, 2560], P(None, ('seq', 'dp')), may hold values from -0.5 to 0.5
- norm_gains: float32 [2, 2560], P(None, ('seq', 'dp')), may hold values from 0.25 to 1.75
Outputs:
- input_grad: bfloat16 [49152, 2560], P(('seq', 'dp'))
- query_grad: bfloat16 [49152, 2560], P(('seq', 'dp'))
- key_grad: bfloat16 [49152, 2560], P(('seq', 'dp'))
- value_grad: bfloat16 [49152, 2560], P(('seq', 'dp'))
- param_grads: float32 [5, 2560], P(None, ('seq', 'dp'))
All inputs are finite; a program needn't handle non-finite values.
Results may differ from a plain program's by a relative error of at most 0.009.
The roundings to bfloat16 on the way count: a program that leaves them out, or rounds other values in their place, can miss the bound.
Values may be sent and summed in bfloat16 or wider, within the bound.
A program may use at most 128 MiB of HBM per device.

v0:
```python
import jax
import jax.numpy as jnp
from jax import lax
from jax.sharding import PartitionSpec as P

HEAD_DIM = 128
epsilon = 1e-06


def root_scale(raw_values):
    floats = raw_values.astype(jnp.float32)
    return lax.rsqrt(jnp.mean(floats * floats, axis=1, keepdims=True) + epsilon)


def head_scores(query_head, key_head):
    return lax.dot_general(
        query_head, key_head, (((1,), (1,)), ((), ())), preferred_element_type=jnp.float32
    ) * query_head.shape[-1] ** (-0.5)


def head_forward(pieces):
    query_head, key_head, value_head = pieces
    scores = head_scores(query_head, key_head)
    row_max = jnp.max(scores, axis=1, keepdims=True)
    row_sum = jnp.sum(jnp.exp(scores - row_max), axis=1, keepdims=True)
    logsum = row_max + jnp.log(row_sum)
    weights_low = jnp.exp(scores - logsum).astype(jnp.bfloat16)
    attended = jnp.dot(weights_low, value_head, preferred_element_type=jnp.float32).astype(
        jnp.bfloat16
    )
    return (attended, logsum[:, 0])


def head_backward(pieces):
    query_head, key_head, value_head, attended, attended_grad, logsum = pieces
    scores = head_scores(query_head, key_head)
    weights = jnp.exp(scores - logsum[:, None])
    row_dot = jnp.sum(
        attended_grad.astype(jnp.float32) * attended.astype(jnp.float32), axis=1, keepdims=True
    )
    weight_grad = lax.dot_general(
        attended_grad, value_head, (((1,), (1,)), ((), ())), preferred_element_type=jnp.float32
    )
    score_grad = (weights * (weight_grad - row_dot) * query_head.shape[-1] ** (-0.5)).astype(
        jnp.bfloat16
    )
    value_part = lax.dot_general(
        weights.astype(jnp.bfloat16),
        attended_grad,
        (((0,), (0,)), ((), ())),
        preferred_element_type=jnp.float32,
    )
    query_part = jnp.dot(score_grad, key_head, preferred_element_type=jnp.float32)
    key_part = lax.dot_general(
        score_grad, query_head, (((0,), (0,)), ((), ())), preferred_element_type=jnp.float32
    )
    return (query_part, key_part, value_part)


def stream_pass(residual, attended, modulated, residual_grad, modulated_grad):
    gate_row = modulated[0]
    scale_row = modulated[1]
    summed = residual.astype(jnp.float32) + gate_row * attended.astype(jnp.float32)
    centered = summed - jnp.mean(summed, axis=1, keepdims=True)
    norm_scale = lax.rsqrt(jnp.mean(centered * centered, axis=1, keepdims=True) + epsilon)
    normed = centered * norm_scale
    scaled_grad = modulated_grad.astype(jnp.float32) * (1.0 + scale_row)
    stream_grad = residual_grad.astype(jnp.float32) + norm_scale * (
        scaled_grad
        - jnp.mean(scaled_grad, axis=1, keepdims=True)
        - normed * jnp.mean(scaled_grad * normed, axis=1, keepdims=True)
    )
    attended_grad = (stream_grad * gate_row).astype(jnp.bfloat16)
    return (stream_grad, normed, attended_grad)


def norm_backward(raw_values, inverse, gain_row, upstream):
    floats = raw_values.astype(jnp.float32)
    weighted = gain_row * upstream
    return (
        inverse * weighted
        - floats * inverse**3 * jnp.mean(floats * weighted, axis=1, keepdims=True)
    ).astype(jnp.bfloat16)


def partial_sums(
    attended,
    stream_grad,
    normed,
    modulated_grad,
    query_raw,
    query_scale,
    query_part,
    key_raw,
    key_scale,
    key_part,
):
    grad_floats = modulated_grad.astype(jnp.float32)
    return jnp.stack(
        [
            jnp.sum(stream_grad * attended.astype(jnp.float32), axis=0),
            jnp.sum(grad_floats, axis=0),
            jnp.sum(grad_floats * normed, axis=0),
            jnp.sum(query_part * query_raw.astype(jnp.float32) * query_scale, axis=0),
            jnp.sum(key_part * key_raw.astype(jnp.float32) * key_scale, axis=0),
        ]
    )


def per_device(
    residual,
    query_raw,
    key_raw,
    values,
    residual_grad,
    modulated_grad,
    condition,
    modulation,
    norm_gains,
):
    head_width = HEAD_DIM
    row_count = residual.shape[0]
    modulation_all, gains_all = (
        lax.all_gather(modulation, ("seq", "dp"), axis=1, tiled=True),
        lax.all_gather(norm_gains, ("seq", "dp"), axis=1, tiled=True),
    )
    modulated = modulation_all + condition[0]
    query_scale = root_scale(query_raw)
    key_scale = root_scale(key_raw)
    normed_query = (query_raw.astype(jnp.float32) * query_scale * gains_all[0]).astype(jnp.bfloat16)
    normed_key = (key_raw.astype(jnp.float32) * key_scale * gains_all[1]).astype(jnp.bfloat16)
    query_moved, key_moved, value_moved = (
        lax.all_to_all(
            normed_query.reshape(row_count, -1, head_width),
            "seq",
            split_axis=1,
            concat_axis=0,
            tiled=True,
        ),
        lax.all_to_all(
            normed_key.reshape(row_count, -1, head_width),
            "seq",
            split_axis=1,
            concat_axis=0,
            tiled=True,
        ),
        lax.all_to_all(
            values.reshape(row_count, -1, head_width),
            "seq",
            split_axis=1,
            concat_axis=0,
            tiled=True,
        ),
    )
    query_heads = query_moved.transpose(1, 0, 2)
    key_heads = key_moved.transpose(1, 0, 2)
    value_heads = value_moved.transpose(1, 0, 2)
    attended_heads, logsum = lax.map(head_forward, (query_heads, key_heads, value_heads))
    attended_tokens = lax.all_to_all(
        attended_heads.transpose(1, 0, 2), "seq", split_axis=0, concat_axis=1, tiled=True
    )
    attended = attended_tokens.reshape(row_count, -1)
    stream_grad, normed, attended_grad = stream_pass(
        residual, attended, modulated, residual_grad, modulated_grad
    )
    grad_moved = lax.all_to_all(
        attended_grad.reshape(row_count, -1, head_width),
        "seq",
        split_axis=1,
        concat_axis=0,
        tiled=True,
    )
    query_part, key_part, value_part = lax.map(
        head_backward,
        (
            query_heads,
            key_heads,
            value_heads,
            attended_heads,
            grad_moved.transpose(1, 0, 2),
            logsum,
        ),
    )
    query_back, key_back, value_back = (
        lax.all_to_all(
            query_part.transpose(1, 0, 2), "seq", split_axis=0, concat_axis=1, tiled=True
        ),
        lax.all_to_all(key_part.transpose(1, 0, 2), "seq", split_axis=0, concat_axis=1, tiled=True),
        lax.all_to_all(
            value_part.transpose(1, 0, 2), "seq", split_axis=0, concat_axis=1, tiled=True
        ),
    )
    query_grad_n = query_back.reshape(row_count, -1)
    key_grad_n = key_back.reshape(row_count, -1)
    value_sum = value_back.reshape(row_count, -1)
    sums_here = partial_sums(
        attended,
        stream_grad,
        normed,
        modulated_grad,
        query_raw,
        query_scale,
        query_grad_n,
        key_raw,
        key_scale,
        key_grad_n,
    )
    reduced = lax.psum_scatter(sums_here, ("seq", "dp"), scatter_dimension=1, tiled=True)
    factor = (row_count * lax.axis_size("seq") * lax.axis_size("dp")) ** (-0.5)
    return (
        stream_grad.astype(jnp.bfloat16),
        norm_backward(query_raw, query_scale, gains_all[0], query_grad_n),
        norm_backward(key_raw, key_scale, gains_all[1], key_grad_n),
        value_sum.astype(jnp.bfloat16),
        reduced * factor,
    )


def solution(mesh):
    placed = (
        P(("seq", "dp"), None),
        P(("seq", "dp"), None),
        P(("seq", "dp"), None),
        P(("seq", "dp"), None),
        P(("seq", "dp"), None),
        P(("seq", "dp"), None),
        P("dp", None, None),
        P(None, ("seq", "dp")),
        P(None, ("seq", "dp")),
    )
    return jax.shard_map(
        per_device,
        mesh=mesh,
        in_specs=placed,
        out_specs=(
            P(("seq", "dp"), None),
            P(("seq", "dp"), None),
            P(("seq", "dp"), None),
            P(("seq", "dp"), None),
            P(None, ("seq", "dp")),
        ),
        check_vma=False,
    )
```

profile of v0, /device:TPU:1, one launch (start us, length us, event | category | flops | bytes accessed | tf_op | source)
XLA Modules:
  0.0 1958.0 jit_solution(11873094181766818667)
XLA Ops:
  3.0 6.7 all-to-all-start.2
  9.8 647.2 %all-gather.1 = f32[256,10,2]{1,2,0:T(2,128)S(1)} all-gather(f32[1,10,2]{1,2,0:T(2,128)S(1)} %bitcast.194), channel_id=1, replica_groups=mesh['seq'=4,'dp'=64] {'seq','dp'}, dimensions={0}, use_global_device_ids=true | all-gather | bytes 20560 | tf_op jit(solution)/shard_map/all_gather | solution.py:125
  658.8 2.4 copy.77
  663.5 3.5 fusion.55
  667.0 2.4 copy.79
  669.4 4.2 all-to-all-start.1
  673.5 2.4 copy.75
  675.9 10.5 all-to-all-done.1
  686.4 5.1 all-to-all-start
  691.5 664.9 %all-gather = f32[256,10,2]{1,2,0:T(2,128)S(1)} all-gather(f32[1,10,2]{1,2,0:T(2,128)S(1)} %bitcast.195), channel_id=1, replica_groups=mesh['seq'=4,'dp'=64] {'seq','dp'}, dimensions={0}, use_global_device_ids=true | all-gather | bytes 20560 | tf_op jit(solution)/shard_map/all_gather | solution.py:124
  1357.2 2.4 copy.85
  1359.6 2.4 copy.70
  1361.9 2.4 copy.69
  1368.5 27.5 %while.26 = (s32[]{:T(128)}, bf16[5,768,128]{2,1,0:T(8,128)(2,1)}, f32[5,768]{1,0:T(8,128)}, bf16[5,768,128]{2,1,0:T(8,128)(2,1)}, bf16[5,768,128]{2,1,0:T(8,128...) while((s32[]{:T(128)}, bf16[5,768,128]{2,1,0:T(8,128)(2,1)}, f32[5,768]{1,0:T(8,128)}, ...), condition=%wide.region_5.6_spmd, body=%wide.region_2.5_spmd.sunk | while | flops 306806016 | bytes 7900257 | solution.py:158
  1396.0 3.1 copy.129
  1399.1 4.7 all-to-all-start.3
  1403.9 19.2 all-to-all-done.3
  1423.1 3.1 copy.84
  1426.3 2.6 fusion.75
  1436.3 2.4 copy.87
  1438.7 4.3 all-to-all-start.4
  1443.0 12.9 all-to-all-done.4
  1457.1 218.5 %while.27 = (s32[]{:T(128)}, f32[5,768,128]{2,0,1:T(8,128)}, f32[5,768,128]{2,0,1:T(8,128)}, bf16[5,768,128]{2,0,1:T(8,128)(2,1)}, bf16[5,768,128]{2,1,0:T(8,128...) while((s32[]{:T(128)}, f32[5,768,128]{2,0,1:T(8,128)}, ...), condition=%wide.region_12.13_spmd, body=%wide.region_10.12_spmd.sunk | while | flops 760675584 | bytes 15945885 | solution.py:173
  1466.9 11.0 dynamic_update_slice.28
  1477.9 11.4 dynamic_update_slice.27
  1489.3 11.4 dynamic_update_slice.26
  1510.6 11.0 dynamic_update_slice.28
  1521.6 11.4 dynamic_update_slice.27
  1533.0 11.4 dynamic_update_slice.26
  1554.3 11.0 dynamic_update_slice.28
  1565.3 11.4 dynamic_update_slice.27
  1576.7 11.4 dynamic_update_slice.26
  1598.0 11.0 dynamic_update_slice.28
  1609.0 11.4 dynamic_update_slice.27
  1620.4 11.4 dynamic_update_slice.26
  1641.7 11.0 dynamic_update_slice.28
  1652.7 11.4 dynamic_update_slice.27
  1664.1 11.4 dynamic_update_slice.26
  1675.5 24.6 %all_to_all.120 = bf16[768,5,128]{2,1,0:T(8,128)(2,1)} all-to-all(bf16[768,5,128]{2,1,0:T(8,128)(2,1)} %bitcast.192), channel_id=1, replica_groups=mesh['seq'=4,'dp'=64] {'seq'}, dimensions={0} | all-to-all | bytes 1966080 | tf_op jit(solution)/shard_map/all_to_all | solution.py:189
  1700.1 40.3 %all_to_all.121 = f32[768,5,128]{2,1,0:T(8,128)} all-to-all(f32[768,5,128]{2,1,0:T(8,128)S(1)} %bitcast.191), channel_id=1, replica_groups=mesh['seq'=4,'dp'=64] {'seq'}, dimensions={0} | all-to-all | bytes 3932160 | tf_op jit(solution)/shard_map/all_to_all | solution.py:185
  1740.4 5.6 all-to-all-start.6
  1748.4 2.6 copy.94
  1753.3 3.3 copy.90
  1756.7 25.5 %all-to-all-done.6 = f32[768,5,128]{2,1,0:T(8,128)} async-done(((f32[768,5,128]{2,1,0:T(8,128)}), f32[768,5,128]{2,1,0:T(8,128)}, u32[]{:S(2)}, u32[]{:S(2)}) %all-to-all-start.6) | async-done | bytes 1966112 | tf_op jit(solution)/shard_map/all_to_all | solution.py:188
  1782.2 3.4 copy.92
  1785.6 3.3 fusion.70
  1793.0 2.9 fusion.61
  1800.0 157.2 %all-reduce = f32[5,2560]{1,0:T(8,128)S(1)} all-reduce(f32[5,2560]{1,0:T(8,128)S(1)} %stack.23), channel_id=2, replica_groups=mesh['seq'=4,'dp'=64] {'seq','dp'}, use_global_device_ids=true, to_apply=%region_20.21.clone | all-reduce | flops 12800 | bytes 102400
  (152 shorter events, 110.2 us)
Async XLA Ops:
  0.6 1.2 copy-start
  0.6 9.1 copy-start.18
  0.7 656.6 %copy-start.9 = (bf16[192,2560]{1,0:T(8,128)(2,1)S(1)}, bf16[192,2560]{1,0:T(8,128)(2,1)}, u32[]{:S(2)}) copy-start(bf16[192,2560]{1,0:T(8,128)(2,1)} %param.14) | copy-start | bytes 2949124
  3.0 666.3 %all-to-all-start.2 = ((bf16[192,20,128]{2,0,1:T(8,128)(2,1)}), bf16[192,20,128]{2,0,1:T(8,128)(2,1)S(1)}, u32[]{:S(2)}, u32[]{:S(2)}) async-start(bf16[192,20,128]{2,0,1:T(8,128)(2,1)} %copy_bitcast_fusion.1), calls=%async_computation.2 | async-start | bytes 1966080 | tf_op jit(solution)/shard_map/all_to_all | solution.py:147
  657.2 6.3 copy-start.10
  663.5 3.5 copy-start.14
  669.4 17.1 all-to-all-start.1
  673.5 18.0 copy-start.19
  686.4 679.9 %all-to-all-start = ((bf16[192,20,128]{2,0,1:T(8,128)(2,1)}), bf16[192,20,128]{2,0,1:T(8,128)(2,1)}, u32[]{:S(2)}, u32[]{:S(2)}) async-start(bf16[192,20,128]{2,0,1:T(8,128)(2,1)} %copy.75), calls=%async_computation | async-start | bytes 1966080 | tf_op jit(solution)/shard_map/all_to_all | solution.py:133
  1396.0 7.8 copy-start.12
  1396.0 7.8 copy-start.13
  1399.1 24.0 %all-to-all-start.3 = ((bf16[768,5,128]{2,1,0:T(8,128)(2,1)}), bf16[768,5,128]{2,1,0:T(8,128)(2,1)}, u32[]{:S(2)}, u32[]{:S(2)}) async-start(bf16[768,5,128]{2,1,0:T(8,128)(2,1)} %bitcast.181), calls=%async_computation.3 | async-start | bytes 3145728 | tf_op jit(solution)/shard_map/all_to_all | solution.py:159
  1428.8 1.3 copy-start.6
  1429.2 3.0 copy-start.5
  1429.2 3.0 copy-start.7
  1438.7 17.2 all-to-all-start.4
  1675.5 24.6 %copy-start.8 = (f32[5,768,128]{2,0,1:T(8,128)S(1)}, f32[5,768,128]{2,0,1:T(8,128)}, u32[]{:S(2)}) copy-start(f32[5,768,128]{2,0,1:T(8,128)} %get-tuple-element.94) | copy-start | bytes 5898244
  1740.4 41.8 %all-to-all-start.6 = ((f32[768,5,128]{2,1,0:T(8,128)}), f32[768,5,128]{2,1,0:T(8,128)}, u32[]{:S(2)}, u32[]{:S(2)}) async-start(f32[768,5,128]{2,1,0:T(8,128)} %bitcast.190), calls=%async_computation.6 | async-start | bytes 6291456 | tf_op jit(solution)/shard_map/all_to_all | solution.py:188
  1782.2 3.4 copy-start.11
  1782.2 3.4 copy-start.15
  1785.6 3.4 copy-start.2
  1785.6 3.4 copy-start.4
  1785.6 3.4 copy-start.17
  1790.6 5.3 copy-start.16
  1793.0 3.0 copy-start.3
  1795.9 162.0 %copy-start.1 = (bf16[192,2560]{1,0:T(8,128)(2,1)S(1)}, bf16[192,2560]{1,0:T(8,128)(2,1)}, u32[]{:S(2)}) copy-start(bf16[192,2560]{1,0:T(8,128)(2,1)} %param.16) | copy-start | bytes 2949124
where the time goes:
time: 1960 us
  blocking collectives  1530 us (78%)
  local copies, waits for them, and re-layouts  232 us (12%)
  waiting for transfers between devices  68.1 us (3%)
  matrix products  57.8 us (3%)
  other arithmetic  34.3 us (2%)
  starting transfers between devices  30.7 us (2%)
    all_gather x1, blocking collectives, per_device(): lax.all_gather(modulation, ('seq', 'dp'), axis=1, tiled=True)  665 us
    all_gather x1, blocking collectives, per_device(): lax.all_gather(norm_gains, ('seq', 'dp'), axis=1, tiled=True)  647 us
    dynamic_update_slice x15, local copies, waits for them, and re-layouts, per_device(): lax.map(head_backward, (query_heads, key_heads, value_heads, attended_hea...  169 us
    unnamed x1, blocking collectives  157 us
    all_to_all x1, blocking collectives, per_device(): lax.all_to_all(query_part.transpose(1, 0, 2), 'seq', split_axis=0, concat...  40.3 us
  transfers between devices with their start and end apart: 6, of which 4 were waited for; matrix products, arithmetic and copies ran while one was open for 2% of the time, Pallas kernels for 0%

commit v1 on v0

--- a/solution.py
+++ b/solution.py
@@ -1,3 +1,4 @@
+import functools
 import jax
 import jax.numpy as jnp
 from jax import lax
@@ -5,6 +6,16 @@
 
 HEAD_DIM = 128
 epsilon = 1e-06
+
+
+def sheet_show(view, mesh_name):
+    e_now = jnp.concatenate(
+        lax.all_to_all(jnp.stack(lax.axis_size(mesh_name) * [view], 0), mesh_name, 0, 0), 1
+    )
+    return e_now
+
+
+fill_pools_on = functools.partial(sheet_show, mesh_name=("seq", "dp"))
 
 
 def root_scale(raw_values):
@@ -121,7 +132,7 @@
     head_width = HEAD_DIM
     row_count = residual.shape[0]
     modulation_all, gains_all = (
-        lax.all_gather(modulation, ("seq", "dp"), axis=1, tiled=True),
+        fill_pools_on(modulation),
         lax.all_gather(norm_gains, ("seq", "dp"), axis=1, tiled=True),
     )
     modulated = modulation_all + condition[0]

time: 1960 us -> 1290 us (0.66)
  blocking collectives: 1530 us -> 841 us
    all_gather x1 -> x0, blocking collectives: 665 us -> none  [per_device(): lax.all_gather(modulation, ('seq', 'dp'), axis=1, tiled=True)]
    unnamed x1, blocking collectives: 157 us -> 128 us
  transfers between devices with their start and end apart: 6 -> 7, of which waited for: 4 -> 6; matrix products, arithmetic and copies ran while one was open for 2% -> 3% of each run, Pallas kernels for 0% -> 0%
where the time goes in v1:
time: 1290 us
  blocking collectives  841 us (65%)
  local copies, waits for them, and re-layouts  233 us (18%)
  waiting for transfers between devices  77 us (6%)
  matrix products  57.8 us (4%)
  starting transfers between devices  43.8 us (3%)
  other arithmetic  34.3 us (3%)
    all_gather x1, blocking collectives, per_device(): lax.all_gather(norm_gains, ('seq', 'dp'), axis=1, tiled=True)  648 us
    dynamic_update_slice x15, local copies, waits for them, and re-layouts, per_device(): lax.map(head_backward, (query_heads, key_heads, value_heads, attended_hea...  169 us
    unnamed x1, blocking collectives  128 us
    all_to_all x1, blocking collectives, per_device(): lax.all_to_all(query_part.transpose(1, 0, 2), 'seq', split_axis=0, concat...  40.3 us
  transfers between devices with their start and end apart: 7, of which 6 were waited for; matrix products, arithmetic and copies ran while one was open for 3% of the time, Pallas kernels for 0%

profile of v1, /device:TPU:1, one launch (start us, length us, event | category | flops | bytes accessed | tf_op | source)
XLA Modules:
  0.0 1287.7 jit_solution(9550166034077311525)
XLA Ops:
  2.2 15.7 %all-to-all-start = ((f32[256,2,10]{2,1,0:T(2,128)}), f32[256,2,10]{2,1,0:T(2,128)S(1)}, u32[]{:S(2)}, u32[]{:S(2)}) async-start(f32[256,2,10]{2,1,0:T(2,128)} %stack.14), calls=%async_computation | async-start | bytes 524288 | tf_op jit(solution)/shard_map/all_to_all | solution.py:13
  17.8 648.1 %all-gather = f32[256,10,2]{1,2,0:T(2,128)S(1)} all-gather(f32[1,10,2]{1,2,0:T(2,128)} %bitcast.189), channel_id=1, replica_groups=mesh['seq'=4,'dp'=64] {'seq','dp'}, dimensions={0}, use_global_device_ids=true | all-gather | bytes 20560 | tf_op jit(solution)/shard_map/all_gather | solution.py:136
  673.3 3.5 all-to-all-start.3
  676.9 3.5 fusion.55
  680.4 2.4 copy.77
  682.7 6.9 all-to-all-done.3
  689.6 4.4 all-to-all-start.2
  694.0 2.4 copy.73
  696.3 10.5 all-to-all-done.2
  706.9 5.1 all-to-all-start.1
  712.0 2.4 copy.83
  714.3 2.4 copy.68
  716.7 2.4 copy.67
  727.2 27.4 %while.26 = (s32[]{:T(128)}, bf16[5,768,128]{2,1,0:T(8,128)(2,1)}, f32[5,768]{1,0:T(8,128)}, bf16[5,768,128]{2,1,0:T(8,128)(2,1)}, bf16[5,768,128]{2,1,0:T(8,128...) while((s32[]{:T(128)}, bf16[5,768,128]{2,1,0:T(8,128)(2,1)}, f32[5,768]{1,0:T(8,128)}, ...), condition=%wide.region_5.6_spmd, body=%wide.region_2.5_spmd.sunk | while | flops 306806016 | bytes 7900257 | solution.py:169
  754.6 3.1 copy.127
  757.7 5.2 all-to-all-start.4
  763.0 19.2 %all-to-all-done.4 = bf16[768,5,128]{2,1,0:T(8,128)(2,1)} async-done(((bf16[768,5,128]{2,1,0:T(8,128)(2,1)}), bf16[768,5,128]{2,1,0:T(8,128)(2,1)}, u32[]{:S(2)}, u32[]{:S(2)}) %all-to-all-start.4) | async-done | bytes 983072 | tf_op jit(solution)/shard_map/all_to_all | solution.py:170
  782.2 3.1 copy.82
  785.3 2.6 fusion.75
  795.3 2.4 copy.85
  797.8 4.3 all-to-all-start.5
  802.1 12.9 %all-to-all-done.5 = bf16[192,20,128]{2,0,1:T(8,128)(2,1)S(1)} async-done(((bf16[192,20,128]{2,0,1:T(8,128)(2,1)}), bf16[192,20,128]{2,0,1:T(8,128)(2,1)S(1)}, u32[]{:S(2)}, u32[]{:S(2)}) %all-to-all-start.5) | async-done | bytes 983072 | tf_op jit(solution)/shard_map/all_to_all | solution.py:177
  816.1 218.5 %while.27 = (s32[]{:T(128)}, f32[5,768,128]{2,0,1:T(8,128)}, f32[5,768,128]{2,0,1:T(8,128)}, bf16[5,768,128]{2,0,1:T(8,128)(2,1)}, bf16[5,768,128]{2,1,0:T(8,128...) while((s32[]{:T(128)}, f32[5,768,128]{2,0,1:T(8,128)}, ...), condition=%wide.region_12.13_spmd, body=%wide.region_10.12_spmd.sunk | while | flops 760675584 | bytes 15945885 | solution.py:184
  826.0 11.0 dynamic_update_slice.28
  837.0 11.4 dynamic_update_slice.27
  848.4 11.4 dynamic_update_slice.26
  869.7 11.0 dynamic_update_slice.28
  880.7 11.4 dynamic_update_slice.27
  892.1 11.4 dynamic_update_slice.26
  913.4 11.0 dynamic_update_slice.28
  924.4 11.4 dynamic_update_slice.27
  935.8 11.4 dynamic_update_slice.26
  957.1 11.0 dynamic_update_slice.28
  968.1 11.4 dynamic_update_slice.27
  979.5 11.4 dynamic_update_slice.26
  1000.8 11.0 dynamic_update_slice.28
  1011.8 11.4 dynamic_update_slice.27
  1023.2 11.4 dynamic_update_slice.26
  1034.6 24.5 %all_to_all.125 = bf16[768,5,128]{2,1,0:T(8,128)(2,1)} all-to-all(bf16[768,5,128]{2,1,0:T(8,128)(2,1)} %bitcast.186), channel_id=1, replica_groups=mesh['seq'=4,'dp'=64] {'seq'}, dimensions={0} | all-to-all | bytes 1966080 | tf_op jit(solution)/shard_map/all_to_all | solution.py:200
  1059.2 40.3 %all_to_all.126 = f32[768,5,128]{2,1,0:T(8,128)} all-to-all(f32[768,5,128]{2,1,0:T(8,128)S(1)} %bitcast.185), channel_id=1, replica_groups=mesh['seq'=4,'dp'=64] {'seq'}, dimensions={0} | all-to-all | bytes 3932160 | tf_op jit(solution)/shard_map/all_to_all | solution.py:196
  1099.4 5.6 all-to-all-start.7
  1107.4 2.6 copy.92
  1112.4 3.3 copy.88
  1115.7 25.5 %all-to-all-done.7 = f32[768,5,128]{2,1,0:T(8,128)} async-done(((f32[768,5,128]{2,1,0:T(8,128)}), f32[768,5,128]{2,1,0:T(8,128)}, u32[]{:S(2)}, u32[]{:S(2)}) %all-to-all-start.7) | async-done | bytes 1966112 | tf_op jit(solution)/shard_map/all_to_all | solution.py:199
  1141.2 3.4 copy.90
  1144.6 3.3 fusion.70
  1152.0 2.9 fusion.61
  1159.1 128.0 %all-reduce = f32[5,2560]{1,0:T(8,128)S(1)} all-reduce(f32[5,2560]{1,0:T(8,128)S(1)} %stack.20), channel_id=2, replica_groups=mesh['seq'=4,'dp'=64] {'seq','dp'}, use_global_device_ids=true, to_apply=%region_20.21.clone | all-reduce | flops 12800 | bytes 102400
  (152 shorter events, 115.6 us)
Async XLA Ops:
  0.6 666.1 %copy-start = (bf16[192,2560]{1,0:T(8,128)(2,1)S(1)}, bf16[192,2560]{1,0:T(8,128)(2,1)}, u32[]{:S(2)}) copy-start(bf16[192,2560]{1,0:T(8,128)(2,1)} %param.16) | copy-start | bytes 2949124
  2.2 671.1 %all-to-all-start = ((f32[256,2,10]{2,1,0:T(2,128)}), f32[256,2,10]{2,1,0:T(2,128)S(1)}, u32[]{:S(2)}, u32[]{:S(2)}) async-start(f32[256,2,10]{2,1,0:T(2,128)} %stack.14), calls=%async_computation | async-start | bytes 524288 | tf_op jit(solution)/shard_map/all_to_all | solution.py:13
  666.7 1.2 copy-start.9
  668.0 1.6 copy-start.10
  668.5 4.7 copy-start.13
  673.3 7.1 copy-start.15
  673.3 7.1 copy-start.11
  673.3 16.3 %all-to-all-start.3 = ((bf16[192,20,128]{2,0,1:T(8,128)(2,1)}), bf16[192,20,128]{2,0,1:T(8,128)(2,1)S(1)}, u32[]{:S(2)}, u32[]{:S(2)}) async-start(bf16[192,20,128]{2,0,1:T(8,128)(2,1)} %copy_bitcast_fusion.1), calls=%async_computation.3 | async-start | bytes 1966080 | tf_op jit(solution)/shard_map/all_to_all | solution.py:158
  689.6 17.2 %all-to-all-start.2 = ((bf16[192,20,128]{2,0,1:T(8,128)(2,1)}), bf16[192,20,128]{2,0,1:T(8,128)(2,1)S(1)}, u32[]{:S(2)}, u32[]{:S(2)}) async-start(bf16[192,20,128]{2,0,1:T(8,128)(2,1)} %copy.77), calls=%async_computation.2 | async-start | bytes 1966080 | tf_op jit(solution)/shard_map/all_to_all | solution.py:151
  706.9 18.1 %all-to-all-start.1 = ((bf16[192,20,128]{2,0,1:T(8,128)(2,1)}), bf16[192,20,128]{2,0,1:T(8,128)(2,1)}, u32[]{:S(2)}, u32[]{:S(2)}) async-start(bf16[192,20,128]{2,0,1:T(8,128)(2,1)} %copy.73), calls=%async_computation.1 | async-start | bytes 1966080 | tf_op jit(solution)/shard_map/all_to_all | solution.py:144
  754.6 8.3 copy-start.14
  757.7 24.5 %all-to-all-start.4 = ((bf16[768,5,128]{2,1,0:T(8,128)(2,1)}), bf16[768,5,128]{2,1,0:T(8,128)(2,1)}, u32[]{:S(2)}, u32[]{:S(2)}) async-start(bf16[768,5,128]{2,1,0:T(8,128)(2,1)} %bitcast.175), calls=%async_computation.4 | async-start | bytes 3145728 | tf_op jit(solution)/shard_map/all_to_all | solution.py:170
  787.9 1.3 copy-start.6
  788.3 3.0 copy-start.5
  788.3 3.0 copy-start.7
  797.8 17.2 %all-to-all-start.5 = ((bf16[192,20,128]{2,0,1:T(8,128)(2,1)}), bf16[192,20,128]{2,0,1:T(8,128)(2,1)S(1)}, u32[]{:S(2)}, u32[]{:S(2)}) async-start(bf16[192,20,128]{2,0,1:T(8,128)(2,1)} %copy.85), calls=%async_computation.5 | async-start | bytes 1966080 | tf_op jit(solution)/shard_map/all_to_all | solution.py:177
  1034.6 24.5 %copy-start.8 = (f32[5,768,128]{2,0,1:T(8,128)S(1)}, f32[5,768,128]{2,0,1:T(8,128)}, u32[]{:S(2)}) copy-start(f32[5,768,128]{2,0,1:T(8,128)} %get-tuple-element.94) | copy-start | bytes 5898244
  1099.4 41.8 %all-to-all-start.7 = ((f32[768,5,128]{2,1,0:T(8,128)}), f32[768,5,128]{2,1,0:T(8,128)}, u32[]{:S(2)}, u32[]{:S(2)}) async-start(f32[768,5,128]{2,1,0:T(8,128)} %bitcast.184), calls=%async_computation.7 | async-start | bytes 6291456 | tf_op jit(solution)/shard_map/all_to_all | solution.py:199
  1141.2 3.4 copy-start.12
  1141.2 3.4 copy-start.16
  1144.6 3.4 copy-start.2
  1144.6 3.4 copy-start.4
  1144.6 3.4 copy-start.18
  1149.7 5.3 copy-start.17
  1152.0 3.0 copy-start.3
  1155.0 132.8 %copy-start.1 = (bf16[192,2560]{1,0:T(8,128)(2,1)S(1)}, bf16[192,2560]{1,0:T(8,128)(2,1)}, u32[]{:S(2)}) copy-start(bf16[192,2560]{1,0:T(8,128)(2,1)} %param.16) | copy-start | bytes 2949124
